TPU v7x, 128 devices: a whole 4x4x4 slice. The times are simulated.
128 devices in a mesh: blk: 16 (over z, y), slab: 2 (over x_hi), micro: 4 (over x_lo, core).
Axes of the slice: x: 4 (x_hi: 2, x_lo: 2; x = x_hi * 2 + x_lo), y: 4, z: 4, core: 2. Of those that a mesh axis runs over, the one named last changes fastest.
Arguments:
- displacement: float32 [128, 128, 256], P('blk', 'micro', 'slab'), may hold values from -6 to 6
- load_field: float32 [128, 128, 256], P('blk', 'micro', 'slab'), may hold values from -6 to 6
- foundation: float32 [128, 128, 256], P('blk', 'micro', 'slab'), may hold values from 0.2 to 2
- plastic_flags: int32 [128, 128, 256], P('blk', 'micro', 'slab'), may hold values 0 or 1
- point_slot: int32 [128, 128, 256], P('blk', 'micro', 'slab'), may hold values from 0 to 65535, as said below
- family_in: float32 [4, 3, 256], replicated, may hold values from -5 to 5
- family_mid: bfloat16 [4, 256, 256], replicated, may hold values from -0.375 to 0.375
- family_out: bfloat16 [4, 3, 256], replicated, may hold values from -0.375 to 0.375
- family_tan: float32 [4, 256], replicated, may hold values from 0.002 to 0.02
Outputs:
- updated_field: float32 [128, 128, 256], P('blk', 'micro', 'slab')
- solver_residual: float32 [128, 128, 256], P('blk', 'micro', 'slab')
Inputs may be any that keep to these rules, and one draw needn't show every extreme that they name: `point_slot`: within each device's block of 8 x 32 x 128 nodes the values are distinct; value // 16384 is the point's fibre family and value % 16384 its position among that family's points of the block in node order (last dimension fastest); in every block one family holds exactly 16384 points.
All inputs are finite; a program needn't handle non-finite values. No bound on the sum of `plastic_flags` on one device may be relied on, other than what follows from the above.
Results may differ from a plain program's by a relative error of at most 0.0024.
Values sent between devices are 32-bit elements; how exact they have to be, the bound alone decides.
A program may use at most 128 MiB of HBM per device.

v0:
```python
import jax
import jax.numpy as jnp
from jax import lax
from jax.sharding import PartitionSpec as P

ITERS = 8


def padded_2(cells, sides, width, closed):
    for axis, dim in sides:
        count = lax.axis_size(axis)
        ends = count if closed else count - 1
        head = lax.slice_in_dim(cells, 0, width, axis=dim)
        tail = lax.slice_in_dim(cells, cells.shape[dim] - width, cells.shape[dim], axis=dim)
        cells = jnp.concatenate(
            [
                lax.ppermute(tail, axis, [(i, (i + 1) % count) for i in range(ends)]),
                cells,
                lax.ppermute(head, axis, [((i + 1) % count, i) for i in range(ends)]),
            ],
            axis=dim,
        )
    return cells


def shifted_diff(extended, dim_index, halo_width, margin, length):
    upper_side = lax.slice_in_dim(
        extended, halo_width - margin + 1, halo_width + length + margin + 1, axis=dim_index
    )
    lower_side = lax.slice_in_dim(
        extended, halo_width - margin - 1, halo_width + length + margin - 1, axis=dim_index
    )
    return (upper_side - lower_side) * 0.5


def extend(stacked, halo_width):
    cycle_ext = padded_2(stacked, (("blk", 1),), halo_width, True)
    slab_ext = padded_2(stacked, (("slab", 3), ("micro", 2)), halo_width, False)
    return (cycle_ext, slab_ext)


def gradients(stacked, halo_width, margin):
    size_x, size_y, size_z = stacked.shape[1:]
    cycle_ext, slab_ext = extend(stacked, halo_width)
    along_x = shifted_diff(cycle_ext, 1, halo_width, margin, size_x)
    along_y = shifted_diff(
        lax.slice_in_dim(slab_ext, halo_width, halo_width + size_z, axis=3),
        2,
        halo_width,
        margin,
        size_y,
    )
    along_z = shifted_diff(
        lax.slice_in_dim(slab_ext, halo_width, halo_width + size_y, axis=2),
        3,
        halo_width,
        margin,
        size_z,
    )
    return (along_x, along_y, along_z)


def fibre_model(block_rows, weight_in, weight_mid, weight_out, weight_tan):
    modal = (
        weight_in[0][:, None] * block_rows[0][None, :]
        + weight_in[1][:, None] * block_rows[1][None, :]
        + weight_in[2][:, None] * block_rows[2][None, :]
    )
    active = jnp.where(block_rows[3][None, :] > 0.5, jnp.tanh(modal), modal).astype(jnp.bfloat16)
    hidden = jnp.dot(weight_mid, active, preferred_element_type=jnp.float32)
    bounded = jnp.tanh(hidden).astype(jnp.bfloat16)
    stress = jnp.dot(weight_out, bounded, preferred_element_type=jnp.float32)
    widened = bounded.astype(jnp.float32)
    tangent = 0.5 + jnp.dot(weight_tan, widened * widened, precision=lax.Precision.HIGHEST)
    return jnp.concatenate([stress, tangent[None, :]], axis=0)


def global_sum(value):
    return lax.psum(value, ("blk", "slab", "micro"))


def body(
    displacement,
    load_field,
    foundation,
    plastic_flags,
    point_slot,
    family_in,
    family_mid,
    family_out,
    family_tan,
):
    size_x, size_y, size_z = displacement.shape
    points_dev = size_x * size_y * size_z
    capacity = points_dev // 2
    family_count = family_in.shape[0]
    strain_x, strain_y, strain_z = gradients(displacement[None], 1, 0)
    payload = jnp.concatenate(
        [strain_x, strain_y, strain_z, plastic_flags[None].astype(jnp.float32)], axis=0
    ).reshape(4, points_dev)
    slots = point_slot.reshape(points_dev)
    padded = (
        jnp.zeros((4, family_count * capacity), jnp.float32)
        .at[:, slots]
        .set(payload)
        .reshape(4, family_count, capacity)
    )
    per_family = lax.map(
        lambda inputs: fibre_model(inputs[0], inputs[1], inputs[2], inputs[3], inputs[4]),
        (jnp.moveaxis(padded, 1, 0), family_in, family_mid, family_out, family_tan),
    )
    returned = jnp.moveaxis(per_family, 0, 1)
    answers = returned.reshape(4, family_count * capacity)[:, slots].reshape(
        4, size_x, size_y, size_z
    )
    cycle_ext, slab_ext = extend(answers, 1)
    stress_x = shifted_diff(cycle_ext[0], 0, 1, 0, size_x)
    stress_y = shifted_diff(slab_ext[1][:, :, 1 : 1 + size_z], 1, 1, 0, size_y)
    stress_z = shifted_diff(slab_ext[2][:, 1 : 1 + size_y, :], 2, 1, 0, size_z)
    tangent_x = cycle_ext[3]
    tangent_y = slab_ext[3][:, :, 1 : 1 + size_z]
    tangent_z = slab_ext[3][:, 1 : 1 + size_y, :]
    rhs = load_field - foundation * displacement + (stress_x + stress_y + stress_z)
    solution = jnp.zeros_like(rhs)
    residual = rhs
    direction = rhs
    current = global_sum(jnp.sum(residual * residual))
    for iteration in range(ITERS):
        grad_x, grad_y, grad_z = gradients(direction[None], 2, 1)
        flux_x = tangent_x * grad_x[0]
        flux_y = tangent_y * grad_y[0]
        flux_z = tangent_z * grad_z[0]
        total = (
            shifted_diff(flux_x, 0, 1, 0, size_x)
            + shifted_diff(flux_y, 1, 1, 0, size_y)
            + shifted_diff(flux_z, 2, 1, 0, size_z)
        )
        image = foundation * direction - total
        alpha = current / global_sum(jnp.sum(direction * image))
        solution = solution + alpha * direction
        residual = residual - alpha * image
        following = global_sum(jnp.sum(residual * residual))
        direction = residual + following / current * direction
        current = following
    return (displacement + solution, residual)


def solution(mesh):
    placed = (
        P("blk", "micro", "slab"),
        P("blk", "micro", "slab"),
        P("blk", "micro", "slab"),
        P("blk", "micro", "slab"),
        P("blk", "micro", "slab"),
        P(),
        P(),
        P(),
        P(),
    )
    return jax.shard_map(
        body,
        mesh=mesh,
        in_specs=placed,
        out_specs=(P("blk", "micro", "slab"), P("blk", "micro", "slab")),
        check_vma=False,
    )
```

profile of v0, /device:TPU:1, one launch (start us, length us, event | category | flops | bytes accessed | tf_op | source)
XLA Modules:
  0.0 1535.5 jit_solution(5746683782115413864)
XLA Ops:
  9.2 6.2 collective-permute-start
  27.0 8.4 copy.40
  35.4 93.5 %scatter_custom_fusion = f32[4,65536]{0,1:T(8,128)} fusion(s32[32768]{0:T(1024)S(1)} %bitcast.213, f32[32768,4]{1,0:T(8,128)} %copy.40, f32[]{:T(128)} %constant.13.clone.1), kind=kCustom, calls=%fused_computation.34 | custom fusion | bytes 1049088 | tf_op jit(solution)/shard_map/scatter | solution.py:105
  128.8 18.1 %copy.41 = f32[4,4,16384]{2,0,1:T(4,128)S(1)} copy(f32[4,4,16384]{0,2,1:T(8,128)} %bitcast.150) | data formatting | bytes 2097152 | tf_op jit(solution)/shard_map/reshape | solution.py:106
  146.9 78.6 %while.10 = (s32[]{:T(128)}, f32[4,4,16384]{2,1,0:T(4,128)S(1)}, bf16[4,3,256]{2,1,0:T(4,128)(2,1)S(1)}, bf16[4,256,256]{2,1,0:T(8,128)(2,1)}, f32[4,4,16384]{2,...) while((s32[]{:T(128)}, f32[4,4,16384]{2,1,0:T(4,128)S(1)}, ...), condition=%wide.region_2.3_spmd, body=%wide.region_1.2_spmd.sunk | while | flops 2265022464 | bytes 26981568 | solution.py:108
  148.2 7.5 fusion.180
  156.9 9.5 fusion.181
  167.7 7.5 fusion.180
  176.4 9.5 fusion.181
  187.2 7.5 fusion.180
  195.9 9.5 fusion.181
  206.7 7.5 fusion.180
  215.4 9.5 fusion.181
  225.5 16.1 %copy.43 = f32[4,4,16384]{0,2,1:T(8,128)} copy(f32[4,4,16384]{2,0,1:T(4,128)S(1)} %bitcast.211) | data formatting | bytes 2097152 | tf_op jit(solution)/shard_map/transpose | solution.py:112
  241.5 119.1 %gather_fusion = f32[32768,4]{1,0:T(8,128)} fusion(f32[4,65536]{0,1:T(8,128)} %bitcast.151, s32[32768]{0:T(1024)S(1)} %broadcast_clamp_fusion), kind=kCustom, calls=%fused_computation | custom fusion | bytes 1179648 | tf_op jit(solution)/shard_map/gather | solution.py:113
  360.6 10.0 copy.45
  378.3 10.2 collective-permute-done.8
  428.5 61.8 %all-reduce = (f32[]{:T(128)}, f32[]{:T(128)}) all-reduce(f32[]{:T(128)} %get-tuple-element.55, f32[]{:T(128)} %get-tuple-element.54), channel_id=1, replica_groups=mesh['blk'=16,'slab'=2,'micro'=4] {'blk','slab','micro'}, use_global_device_ids=true, to_apply=%region_4.5 | all-reduce | flops 2 | bytes 16 | tf_op jit(solution)/shard_map/psum | solution.py:79
  492.3 64.1 %psum.114 = f32[]{:T(128)} all-reduce(f32[]{:T(128)} %multiply_reduce_fusion.13), channel_id=1, replica_groups=mesh['blk'=16,'slab'=2,'micro'=4] {'blk','slab','micro'}, use_global_device_ids=true, to_apply=%region_8.9 | all-reduce | flops 1 | bytes 8 | tf_op jit(solution)/shard_map/psum | solution.py:79
  577.2 62.9 %psum.115 = f32[]{:T(128)} all-reduce(f32[]{:T(128)} %get-tuple-element.96), channel_id=1, replica_groups=mesh['blk'=16,'slab'=2,'micro'=4] {'blk','slab','micro'}, use_global_device_ids=true, to_apply=%region_10.11 | all-reduce | flops 1 | bytes 8 | tf_op jit(solution)/shard_map/psum | solution.py:79
  642.1 62.6 %psum.116 = f32[]{:T(128)} all-reduce(f32[]{:T(128)} %get-tuple-element.94), channel_id=1, replica_groups=mesh['blk'=16,'slab'=2,'micro'=4] {'blk','slab','micro'}, use_global_device_ids=true, to_apply=%region_12.13 | all-reduce | flops 1 | bytes 8 | tf_op jit(solution)/shard_map/psum | solution.py:79
  725.8 62.5 %psum.117 = f32[]{:T(128)} all-reduce(f32[]{:T(128)} %get-tuple-element.92), channel_id=1, replica_groups=mesh['blk'=16,'slab'=2,'micro'=4] {'blk','slab','micro'}, use_global_device_ids=true, to_apply=%region_14.15 | all-reduce | flops 1 | bytes 8 | tf_op jit(solution)/shard_map/psum | solution.py:79
  790.3 63.9 %psum.118 = f32[]{:T(128)} all-reduce(f32[]{:T(128)} %get-tuple-element.90), channel_id=1, replica_groups=mesh['blk'=16,'slab'=2,'micro'=4] {'blk','slab','micro'}, use_global_device_ids=true, to_apply=%region_16.17 | all-reduce | flops 1 | bytes 8 | tf_op jit(solution)/shard_map/psum | solution.py:79
  874.6 63.2 %psum.119 = f32[]{:T(128)} all-reduce(f32[]{:T(128)} %get-tuple-element.88), channel_id=1, replica_groups=mesh['blk'=16,'slab'=2,'micro'=4] {'blk','slab','micro'}, use_global_device_ids=true, to_apply=%region_18.19 | all-reduce | flops 1 | bytes 8 | tf_op jit(solution)/shard_map/psum | solution.py:79
  939.8 62.6 %psum.120 = f32[]{:T(128)} all-reduce(f32[]{:T(128)} %get-tuple-element.86), channel_id=1, replica_groups=mesh['blk'=16,'slab'=2,'micro'=4] {'blk','slab','micro'}, use_global_device_ids=true, to_apply=%region_20.21 | all-reduce | flops 1 | bytes 8 | tf_op jit(solution)/shard_map/psum | solution.py:79
  1023.7 62.4 %psum.121 = f32[]{:T(128)} all-reduce(f32[]{:T(128)} %get-tuple-element.84), channel_id=1, replica_groups=mesh['blk'=16,'slab'=2,'micro'=4] {'blk','slab','micro'}, use_global_device_ids=true, to_apply=%region_22.23 | all-reduce | flops 1 | bytes 8 | tf_op jit(solution)/shard_map/psum | solution.py:79
  1088.2 63.6 %psum.122 = f32[]{:T(128)} all-reduce(f32[]{:T(128)} %get-tuple-element.82), channel_id=1, replica_groups=mesh['blk'=16,'slab'=2,'micro'=4] {'blk','slab','micro'}, use_global_device_ids=true, to_apply=%region_24.25 | all-reduce | flops 1 | bytes 8 | tf_op jit(solution)/shard_map/psum | solution.py:79
  1172.2 63.2 %psum.123 = f32[]{:T(128)} all-reduce(f32[]{:T(128)} %get-tuple-element.80), channel_id=1, replica_groups=mesh['blk'=16,'slab'=2,'micro'=4] {'blk','slab','micro'}, use_global_device_ids=true, to_apply=%region_26.27 | all-reduce | flops 1 | bytes 8 | tf_op jit(solution)/shard_map/psum | solution.py:79
  1237.4 62.6 %psum.124 = f32[]{:T(128)} all-reduce(f32[]{:T(128)} %get-tuple-element.78), channel_id=1, replica_groups=mesh['blk'=16,'slab'=2,'micro'=4] {'blk','slab','micro'}, use_global_device_ids=true, to_apply=%region_28.29 | all-reduce | flops 1 | bytes 8 | tf_op jit(solution)/shard_map/psum | solution.py:79
  1321.2 62.7 %psum.125 = f32[]{:T(128)} all-reduce(f32[]{:T(128)} %get-tuple-element.76), channel_id=1, replica_groups=mesh['blk'=16,'slab'=2,'micro'=4] {'blk','slab','micro'}, use_global_device_ids=true, to_apply=%region_30.31 | all-reduce | flops 1 | bytes 8 | tf_op jit(solution)/shard_map/psum | solution.py:79
  1385.8 63.5 %psum.126 = f32[]{:T(128)} all-reduce(f32[]{:T(128)} %get-tuple-element.74), channel_id=1, replica_groups=mesh['blk'=16,'slab'=2,'micro'=4] {'blk','slab','micro'}, use_global_device_ids=true, to_apply=%region_32.33 | all-reduce | flops 1 | bytes 8 | tf_op jit(solution)/shard_map/psum | solution.py:79
  1469.9 63.2 %psum.127 = f32[]{:T(128)} all-reduce(f32[]{:T(128)} %get-tuple-element.72), channel_id=1, replica_groups=mesh['blk'=16,'slab'=2,'micro'=4] {'blk','slab','micro'}, use_global_device_ids=true, to_apply=%region_34.35 | all-reduce | flops 1 | bytes 8 | tf_op jit(solution)/shard_map/psum | solution.py:79
  (234 shorter events, 218.6 us)
Async XLA Ops:
  1.7 14.8 collective-permute-start.2
  7.2 9.3 collective-permute-start.3
  9.2 15.4 %collective-permute-start = (f32[1,1,32,128]{3,2,1,0:T(8,128)S(1)}, f32[1,1,32,128]{3,2,1,0:T(8,128)S(1)}, u32[]{:S(2)}, u32[]{:S(2)}) collective-permute-start(f32[1,1,32,128]{3,2,1,0:T(8,128)S(1)} %get-tuple-element.169), channel_id=1, source_target_pairs={{8,0},{16,8},{24,16},{32,24},{40,32},{48,40},{56,48},{64,56},{72,6... | collective-permute-start | bytes 49160 | tf_op jit(solution)/shard_map/ppermute | solution.py:19
  15.4 9.2 collective-permute-start.1
  17.4 7.2 collective-permute-start.4
  370.8 17.7 %collective-permute-start.8 = (f32[4,8,32,1]{3,2,1,0:T(8,128)S(1)}, f32[4,8,32,1]{3,2,1,0:T(8,128)S(1)}, u32[]{:S(2)}, u32[]{:S(2)}) collective-permute-start(f32[4,8,32,1]{3,2,1,0:T(8,128)S(1)} %get-tuple-element.114), channel_id=1, source_target_pairs={{0,4},{1,5},{2,6},{3,7},{8,12},{9,13},{10,14},{11,15},{16,20},{17,... | collective-permute-start | bytes 12296 | tf_op jit(solution)/shard_map/ppermute | solution.py:17
  377.0 16.9 %collective-permute-start.9 = (f32[4,8,32,1]{3,2,1,0:T(8,128)S(1)}, f32[4,8,32,1]{3,2,1,0:T(8,128)S(1)}, u32[]{:S(2)}, u32[]{:S(2)}) collective-permute-start(f32[4,8,32,1]{3,2,1,0:T(8,128)S(1)} %get-tuple-element.115), channel_id=1, source_target_pairs={{4,0},{5,1},{6,2},{7,3},{12,8},{13,9},{14,10},{15,11},{20,16},{21,... | collective-permute-start | bytes 12296 | tf_op jit(solution)/shard_map/ppermute | solution.py:19
  394.1 9.5 collective-permute-start.10
  396.1 7.6 collective-permute-start.11
  403.6 7.3 collective-permute-start.7
  412.5 7.8 collective-permute-start.15
  413.8 13.9 collective-permute-start.12
  413.9 13.8 collective-permute-start.13
  561.4 7.2 collective-permute-start.21
  562.7 13.7 collective-permute-start.18
  564.0 12.4 collective-permute-start.19
  709.8 7.5 collective-permute-start.27
  711.1 14.0 collective-permute-start.24
  712.4 12.6 collective-permute-start.25
  860.2 13.7 collective-permute-start.30
  861.8 12.0 collective-permute-start.31
  1007.2 7.5 collective-permute-start.39
  1008.5 14.5 collective-permute-start.36
  1010.2 12.8 collective-permute-start.37
  1014.8 7.2 collective-permute-start.40
  1157.9 13.5 collective-permute-start.42
  1159.4 12.0 collective-permute-start.43
  1304.7 7.5 collective-permute-start.51
  1306.0 14.3 collective-permute-start.48
  1307.9 12.5 collective-permute-start.49
  1455.6 13.5 collective-permute-start.54
  1457.1 12.0 collective-permute-start.55
  (31 other events, 663.6 us)
where the time goes:
time: 1550 us; the launch traced here: 1540 us
  blocking collectives  945 us (61%)
  local copies, waits for them, and re-layouts  272 us (18%)
  starting transfers between devices  136 us (9%)
  matrix products  72.6 us (5%)
  waiting for transfers between devices  64.8 us (4%)
  other arithmetic  22.7 us (1%)
  between operations  22 us (1%)
    psum x15, blocking collectives, global_sum(): return lax.psum(value, ('blk', 'slab', 'micro'))  945 us
    gather x1, local copies, waits for them, and re-layouts, body(): returned.reshape(4, family_count * capacity)[:, slots]  119 us
    scatter x1, local copies, waits for them, and re-layouts, body(): padded = jnp.zeros((4, family_count * capacity), jnp.float32).at[:, slots...  93.5 us
    ppermute x30, starting transfers between devices, padded_2(): lax.ppermute(head, axis, [((i + 1) % count, i) for i in range(ends)])  72.3 us
    ppermute x30, starting transfers between devices, padded_2(): lax.ppermute(tail, axis, [(i, (i + 1) % count) for i in range(ends)])  63.5 us
    ppermute x30, waiting for transfers between devices, padded_2(): lax.ppermute(head, axis, [((i + 1) % count, i) for i in range(ends)])  42.2 us
    dot_general x4, matrix products, fibre_model(): jnp.dot(weight_tan, widened * widened, precision=lax.Precision.HIGHEST)  37.9 us
  transfers between devices with their start and end apart: 60, of which 20 were waited for; matrix products, arithmetic and copies ran while one was open for 1% of the time, Pallas kernels for 0%

commit v1 on v0

--- a/solution.py
+++ b/solution.py
@@ -76,7 +76,7 @@
 
 
 def global_sum(value):
-    return lax.psum(value, ("blk", "slab", "micro"))
+    return jnp.sum(lax.all_gather(value, ("blk", "slab", "micro")), axis=0)
 
 
 def body(

time: 1550 us -> 1570 us (1.013)
    psum x15 -> x0, blocking collectives: 945 us -> none  [global_sum(): return lax.psum(value, ('blk', 'slab', 'micro'))]
    unnamed x0 -> x15, blocking collectives: none -> 943 us
where the time goes in v1:
time: 1570 us; the launch traced here: 1560 us
  blocking collectives  943 us (60%)
  local copies, waits for them, and re-layouts  285 us (18%)
  starting transfers between devices  136 us (9%)
  matrix products  72.6 us (5%)
  waiting for transfers between devices  65 us (4%)
  other arithmetic  32.2 us (2%)
  between operations  22 us (1%)
    unnamed x15, blocking collectives  943 us
    gather x1, local copies, waits for them, and re-layouts, body(): returned.reshape(4, family_count * capacity)[:, slots]  119 us
    scatter x1, local copies, waits for them, and re-layouts, body(): padded = jnp.zeros((4, family_count * capacity), jnp.float32).at[:, slots...  93.5 us
    ppermute x30, starting transfers between devices, padded_2(): lax.ppermute(head, axis, [((i + 1) % count, i) for i in range(ends)])  72.4 us
    ppermute x30, starting transfers between devices, padded_2(): lax.ppermute(tail, axis, [(i, (i + 1) % count) for i in range(ends)])  63.5 us
    ppermute x30, waiting for transfers between devices, padded_2(): lax.ppermute(head, axis, [((i + 1) % count, i) for i in range(ends)])  42.2 us
    dot_general x4, matrix products, fibre_model(): jnp.dot(weight_tan, widened * widened, precision=lax.Precision.HIGHEST)  37.9 us
  transfers between devices with their start and end apart: 60, of which 20 were waited for; matrix products, arithmetic and copies ran while one was open for 1% of the time, Pallas kernels for 0%

profile of v1, /device:TPU:1, one launch (start us, length us, event | category | flops | bytes accessed | tf_op | source)
XLA Modules:
  0.0 1556.7 jit_solution(3632382578997144311)
XLA Ops:
  9.2 6.2 collective-permute-start
  27.0 8.5 copy.40
  35.4 93.5 %scatter_custom_fusion = f32[4,65536]{0,1:T(8,128)} fusion(s32[32768]{0:T(1024)S(1)} %bitcast.229, f32[32768,4]{1,0:T(8,128)} %copy.40, f32[]{:T(128)} %constant.13.clone.1), kind=kCustom, calls=%fused_computation.34 | custom fusion | bytes 1049088 | tf_op jit(solution)/shard_map/scatter | solution.py:105
  128.9 18.1 %copy.41 = f32[4,4,16384]{2,0,1:T(4,128)S(1)} copy(f32[4,4,16384]{0,2,1:T(8,128)} %bitcast.166) | data formatting | bytes 2097152 | tf_op jit(solution)/shard_map/reshape | solution.py:106
  147.0 78.4 %while.10 = (s32[]{:T(128)}, f32[4,4,16384]{2,1,0:T(4,128)S(1)}, bf16[4,3,256]{2,1,0:T(4,128)(2,1)S(1)}, bf16[4,256,256]{2,1,0:T(8,128)(2,1)}, f32[4,4,16384]{2,...) while((s32[]{:T(128)}, f32[4,4,16384]{2,1,0:T(4,128)S(1)}, ...), condition=%wide.region_2.3_spmd, body=%wide.region_1.2_spmd.sunk | while | flops 2265022464 | bytes 26981568 | solution.py:108
  148.3 7.5 fusion.180
  157.0 9.5 fusion.181
  167.8 7.5 fusion.180
  176.5 9.5 fusion.181
  187.3 7.5 fusion.180
  196.0 9.5 fusion.181
  206.8 7.5 fusion.180
  215.5 9.5 fusion.181
  225.4 16.1 %copy.43 = f32[4,4,16384]{0,2,1:T(8,128)} copy(f32[4,4,16384]{2,0,1:T(4,128)S(1)} %bitcast.227) | data formatting | bytes 2097152 | tf_op jit(solution)/shard_map/transpose | solution.py:112
  241.5 118.9 %gather_fusion = f32[32768,4]{1,0:T(8,128)} fusion(f32[4,65536]{0,1:T(8,128)} %bitcast.167, s32[32768]{0:T(1024)S(1)} %broadcast_clamp_fusion), kind=kCustom, calls=%fused_computation | custom fusion | bytes 1179648 | tf_op jit(solution)/shard_map/gather | solution.py:113
  360.4 10.0 copy.45
  378.8 10.6 collective-permute-done.8
  430.6 61.7 %all-reduce.16 = (f32[128]{0:T(128)S(1)}, f32[128]{0:T(128)S(1)}) all-reduce(f32[128]{0:T(128)S(1)} %dynamic-update-slice, f32[128]{0:T(128)S(1)} %dynamic-update-slice.1), channel_id=1, replica_groups=mesh['blk'=16,'slab'=2,'micro'=4] {'blk','slab','micro'}, use_global_device_ids=true, to_apply=%add | all-reduce | flops 256 | bytes 2048
  496.2 64.0 %all-reduce.2 = f32[128]{0:T(128)S(1)} all-reduce(f32[128]{0:T(128)S(1)} %dynamic-update-slice.2), channel_id=1, replica_groups=mesh['blk'=16,'slab'=2,'micro'=4] {'blk','slab','micro'}, use_global_device_ids=true, to_apply=%add.2 | all-reduce | flops 128 | bytes 1024
  582.5 62.4 %all-reduce.3 = f32[128]{0:T(128)S(1)} all-reduce(f32[128]{0:T(128)S(1)} %dynamic-update-slice.3), channel_id=1, replica_groups=mesh['blk'=16,'slab'=2,'micro'=4] {'blk','slab','micro'}, use_global_device_ids=true, to_apply=%add.3 | all-reduce | flops 128 | bytes 1024
  648.3 63.5 %all-reduce.4 = f32[128]{0:T(128)S(1)} all-reduce(f32[128]{0:T(128)S(1)} %dynamic-update-slice.4), channel_id=1, replica_groups=mesh['blk'=16,'slab'=2,'micro'=4] {'blk','slab','micro'}, use_global_device_ids=true, to_apply=%add.4 | all-reduce | flops 128 | bytes 1024
  733.8 63.0 %all-reduce.5 = f32[128]{0:T(128)S(1)} all-reduce(f32[128]{0:T(128)S(1)} %dynamic-update-slice.5), channel_id=1, replica_groups=mesh['blk'=16,'slab'=2,'micro'=4] {'blk','slab','micro'}, use_global_device_ids=true, to_apply=%add.5 | all-reduce | flops 128 | bytes 1024
  800.2 62.6 %all-reduce.6 = f32[128]{0:T(128)S(1)} all-reduce(f32[128]{0:T(128)S(1)} %dynamic-update-slice.6), channel_id=1, replica_groups=mesh['blk'=16,'slab'=2,'micro'=4] {'blk','slab','micro'}, use_global_device_ids=true, to_apply=%add.6 | all-reduce | flops 128 | bytes 1024
  885.3 62.4 %all-reduce.7 = f32[128]{0:T(128)S(1)} all-reduce(f32[128]{0:T(128)S(1)} %dynamic-update-slice.7), channel_id=1, replica_groups=mesh['blk'=16,'slab'=2,'micro'=4] {'blk','slab','micro'}, use_global_device_ids=true, to_apply=%add.7 | all-reduce | flops 128 | bytes 1024
  951.0 63.7 %all-reduce.8 = f32[128]{0:T(128)S(1)} all-reduce(f32[128]{0:T(128)S(1)} %dynamic-update-slice.8), channel_id=1, replica_groups=mesh['blk'=16,'slab'=2,'micro'=4] {'blk','slab','micro'}, use_global_device_ids=true, to_apply=%add.8 | all-reduce | flops 128 | bytes 1024
  1036.6 63.3 %all-reduce.9 = f32[128]{0:T(128)S(1)} all-reduce(f32[128]{0:T(128)S(1)} %dynamic-update-slice.9), channel_id=1, replica_groups=mesh['blk'=16,'slab'=2,'micro'=4] {'blk','slab','micro'}, use_global_device_ids=true, to_apply=%add.9 | all-reduce | flops 128 | bytes 1024
  1103.3 62.6 %all-reduce.10 = f32[128]{0:T(128)S(1)} all-reduce(f32[128]{0:T(128)S(1)} %dynamic-update-slice.10), channel_id=1, replica_groups=mesh['blk'=16,'slab'=2,'micro'=4] {'blk','slab','micro'}, use_global_device_ids=true, to_apply=%add.10 | all-reduce | flops 128 | bytes 1024
  1188.5 62.4 %all-reduce.11 = f32[128]{0:T(128)S(1)} all-reduce(f32[128]{0:T(128)S(1)} %dynamic-update-slice.11), channel_id=1, replica_groups=mesh['blk'=16,'slab'=2,'micro'=4] {'blk','slab','micro'}, use_global_device_ids=true, to_apply=%add.11 | all-reduce | flops 128 | bytes 1024
  1254.3 63.5 %all-reduce.12 = f32[128]{0:T(128)S(1)} all-reduce(f32[128]{0:T(128)S(1)} %dynamic-update-slice.12), channel_id=1, replica_groups=mesh['blk'=16,'slab'=2,'micro'=4] {'blk','slab','micro'}, use_global_device_ids=true, to_apply=%add.12 | all-reduce | flops 128 | bytes 1024
  1339.6 63.2 %all-reduce.13 = f32[128]{0:T(128)S(1)} all-reduce(f32[128]{0:T(128)S(1)} %dynamic-update-slice.13), channel_id=1, replica_groups=mesh['blk'=16,'slab'=2,'micro'=4] {'blk','slab','micro'}, use_global_device_ids=true, to_apply=%add.13 | all-reduce | flops 128 | bytes 1024
  1406.1 62.6 %all-reduce.14 = f32[128]{0:T(128)S(1)} all-reduce(f32[128]{0:T(128)S(1)} %dynamic-update-slice.14), channel_id=1, replica_groups=mesh['blk'=16,'slab'=2,'micro'=4] {'blk','slab','micro'}, use_global_device_ids=true, to_apply=%add.14 | all-reduce | flops 128 | bytes 1024
  1491.4 62.4 %all-reduce.15 = f32[128]{0:T(128)S(1)} all-reduce(f32[128]{0:T(128)S(1)} %dynamic-update-slice.15), channel_id=1, replica_groups=mesh['blk'=16,'slab'=2,'micro'=4] {'blk','slab','micro'}, use_global_device_ids=true, to_apply=%add.15 | all-reduce | flops 128 | bytes 1024
  (282 shorter events, 241.3 us)
Async XLA Ops:
  1.7 14.8 collective-permute-start.2
  7.2 9.3 collective-permute-start.3
  9.2 15.4 collective-permute-start
  15.4 9.2 collective-permute-start.1
  17.4 7.2 collective-permute-start.4
  371.4 18.0 %collective-permute-start.8 = (f32[4,8,32,1]{3,2,1,0:T(8,128)}, f32[4,8,32,1]{3,2,1,0:T(8,128)S(1)}, u32[]{:S(2)}, u32[]{:S(2)}) collective-permute-start(f32[4,8,32,1]{3,2,1,0:T(8,128)} %get-tuple-element.114), channel_id=1, source_target_pairs={{0,4},{1,5},{2,6},{3,7},{8,12},{9,13},{10,14},{11,15},{16,20},{17,... | collective-permute-start | bytes 12296 | tf_op jit(solution)/shard_map/ppermute | solution.py:17
  377.5 16.9 %collective-permute-start.9 = (f32[4,8,32,1]{3,2,1,0:T(8,128)S(1)}, f32[4,8,32,1]{3,2,1,0:T(8,128)S(1)}, u32[]{:S(2)}, u32[]{:S(2)}) collective-permute-start(f32[4,8,32,1]{3,2,1,0:T(8,128)S(1)} %get-tuple-element.115), channel_id=1, source_target_pairs={{4,0},{5,1},{6,2},{7,3},{12,8},{13,9},{14,10},{15,11},{20,16},{21,... | collective-permute-start | bytes 12296 | tf_op jit(solution)/shard_map/ppermute | solution.py:19
  394.7 9.5 collective-permute-start.10
  396.6 7.6 collective-permute-start.11
  404.2 7.3 collective-permute-start.7
  413.1 7.8 collective-permute-start.15
  414.4 13.9 collective-permute-start.12
  414.5 13.8 collective-permute-start.13
  565.9 7.2 collective-permute-start.21
  567.2 13.8 collective-permute-start.18
  568.5 12.5 collective-permute-start.19
  718.8 13.5 collective-permute-start.24
  720.1 12.2 collective-permute-start.25
  868.1 7.5 collective-permute-start.33
  869.4 14.3 collective-permute-start.30
  871.1 12.6 collective-permute-start.31
  1021.4 13.7 collective-permute-start.36
  1023.1 12.1 collective-permute-start.37
  1171.2 7.5 collective-permute-start.45
  1172.6 14.5 collective-permute-start.42
  1174.3 12.8 collective-permute-start.43
  1324.6 13.5 collective-permute-start.48
  1326.0 12.0 collective-permute-start.49
  1474.0 7.5 collective-permute-start.57
  1475.3 14.5 collective-permute-start.54
  1477.1 12.8 collective-permute-start.55
  1481.7 7.3 collective-permute-start.58
  (31 other events, 666.0 us)
